TPU v7x, 256 devices: a whole 4x4x8 slice. The times are simulated.
256 devices in a mesh: occ: 32 (over z, x_hi, core), vir: 8 (over x_lo, y).
Axes of the slice: x: 4 (x_hi: 2, x_lo: 2; x = x_hi * 2 + x_lo), y: 4, z: 8, core: 2. Of those that a mesh axis runs over, the one named last changes fastest.
Arguments:
- factors: bfloat16 [32, 1024, 3072], P('occ', 'vir'), may hold values from -0.71875 to 0.71875
- occ_energy: float32 [32], replicated, may hold values from -2 to -0.4
- vir_energy: float32 [1024], replicated, may hold values from 0.4 to 4
- density_in: float32 [32, 1024, 3072], P('occ', 'vir'), may hold values from -3 to 3
Outputs:
- density: float32 [32, 1024, 3072], P('occ', 'vir')
All inputs are finite; a program needn't handle non-finite values.
Results may differ from a plain program's by a relative error of at most 0.0027.
Values may be sent and summed in bfloat16 or wider, within the bound.
No kernel may reach another device: no remote copies, remote signals or barrier semaphores. Data moves between devices by JAX's collectives and lax.ppermute only.
A program may use at most 128 MiB of HBM per device.

v0:
```python
import jax
import jax.numpy as jnp
from jax import lax
from jax.sharding import PartitionSpec as P

VISITS = 3


def passed_along(block, axis, distance):
    devices = range(lax.axis_size(axis))
    route = [((i - distance) % len(devices), i) for i in devices]
    return lax.ppermute(block, axis, route)


def on_device(factors, occ_energy, vir_energy, density_in):
    occ_rows = factors.shape[0]
    vir_local = factors.shape[1]
    aux_width = factors.shape[2]
    vir_whole = vir_energy.shape[0]
    occ_rank = lax.axis_index("occ")
    cycle_size = lax.axis_size("occ")
    vir_rank = lax.axis_index("vir")
    e_own = lax.dynamic_slice_in_dim(occ_energy, occ_rank * occ_rows, occ_rows, 0)
    e_local = lax.dynamic_slice_in_dim(vir_energy, vir_rank * vir_local, vir_local, 0)
    flat_own = factors.reshape(occ_rows * vir_local, aux_width)
    total = density_in.reshape(occ_rows * vir_local, aux_width)
    partner_shard = factors
    partner = factors
    for visit in range(VISITS):
        if visit > 0:
            partner_shard = passed_along(partner_shard, "occ", 1)
        partner = lax.all_gather(partner_shard, "vir", axis=1, tiled=True)
        other = (occ_rank - visit) % cycle_size * occ_rows
        e_partner = lax.dynamic_slice_in_dim(occ_energy, other, occ_rows, 0)
        flat_partner = partner.reshape(occ_rows * vir_whole, aux_width)
        direct = lax.dot_general(
            flat_own, flat_partner, (((1,), (1,)), ((), ())), preferred_element_type=jnp.float32
        )
        direct = direct.astype(jnp.bfloat16).reshape(occ_rows, vir_local, occ_rows, vir_whole)
        swapped = lax.all_to_all(direct, "vir", split_axis=3, concat_axis=1, tiled=True).transpose(
            0, 3, 2, 1
        )
        denom = (
            e_own[:, None, None, None]
            + e_partner[None, None, :, None]
            - e_local[None, :, None, None]
            - vir_energy[None, None, None, :]
        )
        amp = ((2.0 * direct.astype(jnp.float32) - swapped.astype(jnp.float32)) / denom).astype(
            jnp.bfloat16
        )
        total = total + jnp.dot(
            amp.reshape(occ_rows * vir_local, occ_rows * vir_whole),
            flat_partner,
            preferred_element_type=jnp.float32,
        )
    return total.reshape(density_in.shape)


def solution(mesh):
    return jax.shard_map(
        on_device,
        mesh=mesh,
        in_specs=(P("occ", "vir", None), P(), P(), P("occ", "vir", None)),
        out_specs=P("occ", "vir", None),
        check_vma=False,
    )
```

profile of v0, /device:TPU:4, one launch (start us, length us, event | category | flops | bytes accessed | tf_op | source)
XLA Modules:
  0.0 283.8 jit_solution(7729517185686654184)
XLA Ops:
  6.5 0.0 copy-start.4
  6.5 0.0 copy-start.3
  6.5 0.0 all-gather.4.cloned.1.call-start
  6.5 0.7 all-gather.4.cloned.1.call-update
  7.3 0.0 all-gather.6.cloned.1.call-start
  7.3 0.1 collective-permute-start
  7.4 13.1 %collective-permute-done = bf16[1,128,3072]{2,1,0:T(8,128)(2,1)S(1)} collective-permute-done((bf16[1,128,3072]{2,1,0:T(8,128)(2,1)}, bf16[1,128,3072]{2,1,0:T(8,128)(2,1)S(1)}, u32[]{:S(2)}, u32[]{:S(2)}) %collective-permute-start) | collective-permute-done | bytes 786464 | tf_op jit(solution)/shard_map/ppermute | solution.py:12
  20.5 0.0 copy-start.2
  20.5 0.9 copy-done.2
  21.4 0.0 all-gather.6.cloned.1.call-update
  21.4 0.0 all-gather.8.cloned.1.call-start
  21.5 0.1 collective-permute-start.1
  21.6 29.9 %collective-permute-done.1 = bf16[1,128,3072]{2,1,0:T(8,128)(2,1)S(1)} collective-permute-done((bf16[1,128,3072]{2,1,0:T(8,128)(2,1)}, bf16[1,128,3072]{2,1,0:T(8,128)(2,1)S(1)}, u32[]{:S(2)}, u32[]{:S(2)}) %collective-permute-start.1) | collective-permute-done | bytes 786464 | tf_op jit(solution)/shard_map/ppermute | solution.py:12
  51.4 0.0 copy-start.1
  51.4 0.9 copy-done.1
  52.3 0.0 all-gather.8.cloned.1.call-update
  52.3 0.0 copy-start
  52.3 42.7 %all-gather.4.cloned.1.call-done = bf16[1,1024,3072]{2,1,0:T(8,128)(2,1)} async-done(((bf16[1,128,3072]{2,1,0:T(8,128)(2,1)}), bf16[1,1024,3072]{2,1,0:T(8,128)(2,1)}) %all-gather.4.cloned.1.call-update) | async-done | bytes 6291472 | tf_op jit(solution)/shard_map/all_gather | solution.py:32
  95.1 5.3 %fusion.24 = bf16[128,1024]{1,0:T(8,128)(2,1)S(1)} fusion(bf16[1,1024,3072]{2,1,0:T(8,128)(2,1)} %all-gather.4.cloned.1.call-done, bf16[1,128,3072]{2,1,0:T(8,128)(2,1)} %param.4), kind=kOutput, calls=%fused_computation.16 | convolution fusion | flops 805437440 | bytes 7340032 | tf_op jit(solution)/shard_map/dot_general | solution.py:36
  100.3 0.4 copy.8
  100.7 0.6 broadcast.152
  101.3 2.2 reduce
  103.6 0.8 reshape.223
  104.4 3.4 %all-to-all-start = ((bf16[8,2,8192]{2,1,0:T(2,128)(2,1)}), bf16[8,2,8192]{2,1,0:T(2,128)(2,1)S(1)}, u32[]{:S(2)}, u32[]{:S(2)}) async-start(bf16[8,2,8192]{2,1,0:T(2,128)(2,1)} %reshape.223), calls=%async_computation | async-start | bytes 524288 | tf_op jit(solution)/shard_map/all_to_all | solution.py:40
  107.8 0.0 copy-done.4
  107.8 0.7 fusion.57
  112.2 0.0 copy-done.3
  112.2 0.1 broadcast_subtract_fusion
  112.3 6.5 %all-to-all-done = bf16[8,2,8192]{2,1,0:T(2,128)(2,1)S(1)} async-done(((bf16[8,2,8192]{2,1,0:T(2,128)(2,1)}), bf16[8,2,8192]{2,1,0:T(2,128)(2,1)S(1)}, u32[]{:S(2)}, u32[]{:S(2)}) %all-to-all-start) | async-done | bytes 262176 | tf_op jit(solution)/shard_map/all_to_all | solution.py:40
  118.8 0.3 reshape.224
  119.0 0.5 bitcast_convert_fusion.2
  119.6 0.3 copy.19
  119.9 0.1 reshape.217
  120.0 53.0 %all-gather.6.cloned.1.call-done = bf16[1,1024,3072]{2,1,0:T(8,128)(2,1)} async-done(((bf16[1,128,3072]{2,1,0:T(8,128)(2,1)}), bf16[1,1024,3072]{2,1,0:T(8,128)(2,1)}) %all-gather.6.cloned.1.call-update) | async-done | bytes 6291472 | tf_op jit(solution)/shard_map/all_gather | solution.py:32
  173.0 0.0 copy-done
  173.0 5.0 %fusion.27 = bf16[128,1024]{1,0:T(8,128)(2,1)S(1)} fusion(bf16[1,1024,3072]{2,1,0:T(8,128)(2,1)} %all-gather.6.cloned.1.call-done, bf16[1,128,3072]{2,1,0:T(8,128)(2,1)S(1)} %copy-done), kind=kOutput, calls=%fused_computation.17 | convolution fusion | flops 805437440 | bytes 7340032 | tf_op jit(solution)/shard_map/dot_general | solution.py:36
  178.0 0.4 copy.10
  178.4 2.3 reduce.1
  180.7 0.8 reshape.225
  181.5 4.2 %all-to-all-start.1 = ((bf16[8,2,8192]{2,1,0:T(2,128)(2,1)}), bf16[8,2,8192]{2,1,0:T(2,128)(2,1)}, u32[]{:S(2)}, u32[]{:S(2)}) async-start(bf16[8,2,8192]{2,1,0:T(2,128)(2,1)} %reshape.225), calls=%async_computation.1 | async-start | bytes 524288 | tf_op jit(solution)/shard_map/all_to_all | solution.py:40
  185.7 4.4 %fusion.12 = f32[128,3072]{1,0:T(8,128)S(1)} fusion(bf16[1,1024,3072]{2,1,0:T(8,128)(2,1)} %all-gather.4.cloned.1.call-done, f32[1,128,3072]{2,1,0:T(8,128)} %param.7, f32[1,1024,1,128]{1,3,2,0:T(8,128)S(1)} %reshape.217, bf16[128,1024]{1,0:T(8,128)(2,1)S(1)} %fusion.24, f32[1024]{0:T(1024)S(1)} %copy-done.3, f32[128]{0:T(128)S(1)} %get-tuple-element.7), kind=kOutput, calls=%fused_computation.12 | convolution fusion | flops 806486016 | bytes 10228224 | tf_op jit(solution)/shard_map/dot_general | solution.py:52
  190.1 6.5 %all-to-all-done.1 = bf16[8,2,8192]{2,1,0:T(2,128)(2,1)} async-done(((bf16[8,2,8192]{2,1,0:T(2,128)(2,1)}), bf16[8,2,8192]{2,1,0:T(2,128)(2,1)}, u32[]{:S(2)}, u32[]{:S(2)}) %all-to-all-start.1) | async-done | bytes 262176 | tf_op jit(solution)/shard_map/all_to_all | solution.py:40
  196.5 1.2 reshape.226
  197.7 0.5 bitcast_convert_fusion.1
  198.3 1.1 copy.18
  199.4 1.1 reshape.218
  200.5 50.8 %all-gather.8.cloned.1.call-done = bf16[1,1024,3072]{2,1,0:T(8,128)(2,1)} async-done(((bf16[1,128,3072]{2,1,0:T(8,128)(2,1)}), bf16[1,1024,3072]{2,1,0:T(8,128)(2,1)}) %all-gather.8.cloned.1.call-update) | async-done | bytes 6291472 | tf_op jit(solution)/shard_map/all_gather | solution.py:32
  251.3 5.0 %fusion.30 = bf16[128,1024]{1,0:T(8,128)(2,1)S(1)} fusion(bf16[1,1024,3072]{2,1,0:T(8,128)(2,1)} %all-gather.8.cloned.1.call-done, bf16[1,128,3072]{2,1,0:T(8,128)(2,1)S(1)} %copy-done), kind=kOutput, calls=%fused_computation.18 | convolution fusion | flops 805437440 | bytes 7340032 | tf_op jit(solution)/shard_map/dot_general | solution.py:36
  256.3 0.4 copy.12
  256.7 2.3 reduce.2
  258.9 0.8 reshape.227
  259.7 3.4 %all-to-all-start.2 = ((bf16[8,2,8192]{2,1,0:T(2,128)(2,1)}), bf16[8,2,8192]{2,1,0:T(2,128)(2,1)S(1)}, u32[]{:S(2)}, u32[]{:S(2)}) async-start(bf16[8,2,8192]{2,1,0:T(2,128)(2,1)} %reshape.227), calls=%async_computation.2 | async-start | bytes 524288 | tf_op jit(solution)/shard_map/all_to_all | solution.py:40
  263.1 5.0 %fusion.15 = f32[128,3072]{1,0:T(8,128)} fusion(f32[128,3072]{1,0:T(8,128)S(1)} %fusion.12, bf16[1,1024,3072]{2,1,0:T(8,128)(2,1)} %all-gather.6.cloned.1.call-done, f32[1,1024,1,128]{1,3,2,0:T(8,128)S(1)} %reshape.218, bf16[128,1024]{1,0:T(8,128)(2,1)S(1)} %fusion.27, f32[128]{0:T(128)S(1)} %get-tuple-element.6, f32[1024]{0:T(1024)S(1)} %copy-done.3), kind=kOutput, calls=%fused_computation.13 | convolution fusion | flops 806486016 | bytes 10228224 | tf_op jit(solution)/shard_map/dot_general | solution.py:52
  268.2 2.4 all-to-all-done.2
  270.6 0.3 reshape.228
  270.8 0.5 bitcast_convert_fusion
  271.4 0.3 copy.17
  271.7 0.1 reshape.219
  271.8 5.5 %fusion.21 = f32[1,128,3072]{2,1,0:T(8,128)} fusion(f32[128,3072]{1,0:T(8,128)} %fusion.15, bf16[1,1024,3072]{2,1,0:T(8,128)(2,1)} %all-gather.8.cloned.1.call-done, f32[1,1024,1,128]{1,3,2,0:T(8,128)S(1)} %reshape.219, bf16[128,1024]{1,0:T(8,128)(2,1)S(1)} %fusion.30, f32[128]{0:T(128)S(1)} %get-tuple-element.5, f32[1024]{0:T(1024)S(1)} %copy-done.3), kind=kOutput, calls=%fused_computation.15 | convolution fusion | flops 806486016 | bytes 10228224 | tf_op jit(solution)/shard_map/dot_general | solution.py:52
Async XLA Ops:
  6.5 101.3 %copy-start.4 = (f32[32]{0:T(128)S(1)}, f32[32]{0:T(128)}, u32[]{:S(2)}) copy-start(f32[32]{0:T(128)} %param.5) | copy-start | bytes 388
  6.5 105.7 %copy-start.3 = (f32[1024]{0:T(1024)S(1)}, f32[1024]{0:T(1024)}, u32[]{:S(2)}) copy-start(f32[1024]{0:T(1024)} %param.6) | copy-start | bytes 12292
  6.5 88.5 %all-gather.4.cloned.1.call-start = ((), (), s32[]{:S(2)}) async-start(), calls=%async_computation.3 | async-start | bytes 7077888 | tf_op jit(solution)/shard_map/all_gather | solution.py:32
  7.3 165.8 %all-gather.6.cloned.1.call-start = ((), (), s32[]{:S(2)}) async-start(), calls=%async_computation.4 | async-start | bytes 7077888 | tf_op jit(solution)/shard_map/all_gather | solution.py:32
  7.3 13.2 %collective-permute-start = (bf16[1,128,3072]{2,1,0:T(8,128)(2,1)}, bf16[1,128,3072]{2,1,0:T(8,128)(2,1)S(1)}, u32[]{:S(2)}, u32[]{:S(2)}) collective-permute-start(bf16[1,128,3072]{2,1,0:T(8,128)(2,1)} %param.4), channel_id=1, source_target_pairs={{248,0},{0,8},{8,16},{16,24},{24,32},{32,40},{40,48},{48,56},{56,6... | collective-permute-start | bytes 2359304 | tf_op jit(solution)/shard_map/ppermute | solution.py:12
  20.5 0.9 copy-start.2
  21.4 229.9 %all-gather.8.cloned.1.call-start = ((), (), s32[]{:S(2)}) async-start(), calls=%async_computation.5 | async-start | bytes 7077888 | tf_op jit(solution)/shard_map/all_gather | solution.py:32
  21.5 29.9 %collective-permute-start.1 = (bf16[1,128,3072]{2,1,0:T(8,128)(2,1)}, bf16[1,128,3072]{2,1,0:T(8,128)(2,1)S(1)}, u32[]{:S(2)}, u32[]{:S(2)}) collective-permute-start(bf16[1,128,3072]{2,1,0:T(8,128)(2,1)} %copy-done.2), channel_id=1, source_target_pairs={{248,0},{0,8},{8,16},{16,24},{24,32},{32,40},{40,48},{48,56},{56,6... | collective-permute-start | bytes 2359304 | tf_op jit(solution)/shard_map/ppermute | solution.py:12
  51.4 0.9 copy-start.1
  52.3 120.7 %copy-start = (bf16[1,128,3072]{2,1,0:T(8,128)(2,1)S(1)}, bf16[1,128,3072]{2,1,0:T(8,128)(2,1)}, u32[]{:S(2)}) copy-start(bf16[1,128,3072]{2,1,0:T(8,128)(2,1)} %param.4) | copy-start | bytes 2359300
  104.4 14.4 %all-to-all-start = ((bf16[8,2,8192]{2,1,0:T(2,128)(2,1)}), bf16[8,2,8192]{2,1,0:T(2,128)(2,1)S(1)}, u32[]{:S(2)}, u32[]{:S(2)}) async-start(bf16[8,2,8192]{2,1,0:T(2,128)(2,1)} %reshape.223), calls=%async_computation | async-start | bytes 524288 | tf_op jit(solution)/shard_map/all_to_all | solution.py:40
  181.5 15.1 %all-to-all-start.1 = ((bf16[8,2,8192]{2,1,0:T(2,128)(2,1)}), bf16[8,2,8192]{2,1,0:T(2,128)(2,1)}, u32[]{:S(2)}, u32[]{:S(2)}) async-start(bf16[8,2,8192]{2,1,0:T(2,128)(2,1)} %reshape.225), calls=%async_computation.1 | async-start | bytes 524288 | tf_op jit(solution)/shard_map/all_to_all | solution.py:40
  259.7 10.8 %all-to-all-start.2 = ((bf16[8,2,8192]{2,1,0:T(2,128)(2,1)}), bf16[8,2,8192]{2,1,0:T(2,128)(2,1)S(1)}, u32[]{:S(2)}, u32[]{:S(2)}) async-start(bf16[8,2,8192]{2,1,0:T(2,128)(2,1)} %reshape.227), calls=%async_computation.2 | async-start | bytes 524288 | tf_op jit(solution)/shard_map/all_to_all | solution.py:40
Sparse Core Ops, SparseCore 0:
  9.1 85.8 all-gather.3
  96.8 76.1 all-gather.5
  174.8 76.4 all-gather.7
where the time goes:
time: 284 us
  waiting for transfers between devices  206 us (73%)
  matrix products  30.1 us (11%)
  between operations  17.1 us (6%)
  local copies, waits for them, and re-layouts  11.3 us (4%)
  starting transfers between devices  11.3 us (4%)
  other arithmetic  8.46 us (3%)
    all_gather x3, waiting for transfers between devices, on_device(): partner = lax.all_gather(partner_shard, 'vir', axis=1, tiled=True)  147 us
    ppermute x2, waiting for transfers between devices, passed_along(): return lax.ppermute(block, axis, route)  43 us
    all_to_all x3, waiting for transfers between devices, on_device(): lax.all_to_all(direct, 'vir', split_axis=3, concat_axis=1, tiled=True)  15.3 us
    dot_general x3, matrix products, on_device(): lax.dot_general(flat_own, flat_partner, (((1,), (1,)), ((), ())), preferr...  15.2 us
    dot_general x3, matrix products, on_device(): jnp.dot(amp.reshape(occ_rows * vir_local, occ_rows * vir_whole), flat_par...  14.9 us
    all_to_all x3, starting transfers between devices, on_device(): lax.all_to_all(direct, 'vir', split_axis=3, concat_axis=1, tiled=True)  11 us
    unnamed x3, other arithmetic  6.75 us
    unnamed x17, local copies, waits for them, and re-layouts  6.4 us
  transfers between devices with their start and end apart: 8, of which 8 were waited for; matrix products, arithmetic and copies ran while one was open for 12% of the time, Pallas kernels for 0%

commit v1 on v0

--- a/solution.py
+++ b/solution.py
@@ -29,7 +29,9 @@
     for visit in range(VISITS):
         if visit > 0:
             partner_shard = passed_along(partner_shard, "occ", 1)
-        partner = lax.all_gather(partner_shard, "vir", axis=1, tiled=True)
+        partner = jnp.concatenate(
+            lax.all_to_all(jnp.stack([partner_shard] * lax.axis_size("vir")), "vir", 0, 0), axis=1
+        )
         other = (occ_rank - visit) % cycle_size * occ_rows
         e_partner = lax.dynamic_slice_in_dim(occ_energy, other, occ_rows, 0)
         flat_partner = partner.reshape(occ_rows * vir_whole, aux_width)

time: 284 us -> 305 us (1.074)
  starting transfers between devices: 11.3 us -> 29.1 us
  between operations: 17.1 us -> 3.74 us
  local copies, waits for them, and re-layouts: 11.3 us -> 22 us
    all_gather x3 -> x0, waiting for transfers between devices: 147 us -> none  [on_device(): partner = lax.all_gather(partner_shard, 'vir', axis=1, tiled=True)]
    all_to_all x0 -> x3, waiting for transfers between devices: none -> 122 us  [on_device(): lax.all_to_all(jnp.stack([partner_shard] * lax.axis_size('vir')), 'vir',...]
    ppermute x2, waiting for transfers between devices: 43 us -> 77.2 us  [passed_along(): return lax.ppermute(block, axis, route)]
    all_to_all x0 -> x3, starting transfers between devices: none -> 15.4 us  [on_device(): lax.all_to_all(jnp.stack([partner_shard] * lax.axis_size('vir')), 'vir',...]
    another operation x0 -> x3, local copies, waits for them, and re-layouts: none -> 12.7 us  [on_device(): jnp.stack([partner_shard] * lax.axis_size('vir'))]
    all_to_all x3, waiting for transfers between devices: 15.3 us -> 9.58 us  [on_device(): lax.all_to_all(direct, 'vir', split_axis=3, concat_axis=1, tiled=True)]
    unnamed x17 -> x15, local copies, waits for them, and re-layouts: 6.4 us -> 4.52 us
  transfers between devices with their start and end apart: 8 -> 8, of which waited for: 8 -> 6; matrix products, arithmetic and copies ran while one was open for 12% -> 11% of each run, Pallas kernels for 0% -> 0%
where the time goes in v1:
time: 305 us; the launch traced here: 302 us
  waiting for transfers between devices  209 us (69%)
  matrix products  29.8 us (10%)
  starting transfers between devices  29.1 us (10%)
  local copies, waits for them, and re-layouts  22 us (7%)
  other arithmetic  8.24 us (3%)
  between operations  3.74 us (1%)
    all_to_all x3, waiting for transfers between devices, on_device(): lax.all_to_all(jnp.stack([partner_shard] * lax.axis_size('vir')), 'vir',...  122 us
    ppermute x2, waiting for transfers between devices, passed_along(): return lax.ppermute(block, axis, route)  77.2 us
    all_to_all x3, starting transfers between devices, on_device(): lax.all_to_all(jnp.stack([partner_shard] * lax.axis_size('vir')), 'vir',...  15.4 us
    dot_general x3, matrix products, on_device(): lax.dot_general(flat_own, flat_partner, (((1,), (1,)), ((), ())), preferr...  14.9 us
    dot_general x3, matrix products, on_device(): jnp.dot(amp.reshape(occ_rows * vir_local, occ_rows * vir_whole), flat_par...  14.9 us
    all_to_all x3, starting transfers between devices, on_device(): lax.all_to_all(direct, 'vir', split_axis=3, concat_axis=1, tiled=True)  13.6 us
    another operation x3, local copies, waits for them, and re-layouts, on_device(): jnp.stack([partner_shard] * lax.axis_size('vir'))  12.7 us
    all_to_all x3, waiting for transfers between devices, on_device(): lax.all_to_all(direct, 'vir', split_axis=3, concat_axis=1, tiled=True)  9.58 us
  transfers between devices with their start and end apart: 8, of which 6 were waited for; matrix products, arithmetic and copies ran while one was open for 11% of the time, Pallas kernels for 0%

profile of v1, /device:TPU:4, one launch (start us, length us, event | category | flops | bytes accessed | tf_op | source)
XLA Modules:
  0.0 302.1 jit_solution(9908088125168099960)
XLA Ops:
  0.0 4.6 %stack.6 = bf16[8,1,128,3072]{3,2,1,0:T(8,128)(2,1)} broadcast(bf16[128,3072]{1,0:T(8,128)(2,1)} %bitcast.112), dimensions={2,3} | broadcast | bytes 7077888 | tf_op jit(solution)/shard_map/stack | solution.py:33
  4.6 0.0 copy-start
  4.6 5.2 %all-to-all-start = ((bf16[8,1,128,3072]{3,2,1,0:T(8,128)(2,1)}), bf16[8,1,128,3072]{3,2,1,0:T(8,128)(2,1)}, u32[]{:S(2)}, u32[]{:S(2)}) async-start(bf16[8,1,128,3072]{3,2,1,0:T(8,128)(2,1)} %stack.6), calls=%async_computation | async-start | bytes 12582912 | tf_op jit(solution)/shard_map/all_to_all | solution.py:33
  9.9 0.0 copy-done
  9.9 0.1 collective-permute-start
  10.0 77.2 %collective-permute-done = bf16[1,128,3072]{2,1,0:T(8,128)(2,1)S(1)} collective-permute-done((bf16[1,128,3072]{2,1,0:T(8,128)(2,1)S(1)}, bf16[1,128,3072]{2,1,0:T(8,128)(2,1)S(1)}, u32[]{:S(2)}, u32[]{:S(2)}) %collective-permute-start) | collective-permute-done | bytes 786464 | tf_op jit(solution)/shard_map/ppermute | solution.py:12
  87.2 1.1 all-to-all-done
  88.3 3.4 %stack.7 = bf16[8,1,128,3072]{3,2,1,0:T(8,128)(2,1)} broadcast(bf16[128,3072]{1,0:T(8,128)(2,1)S(1)} %bitcast.125), dimensions={2,3} | broadcast | bytes 7077888 | tf_op jit(solution)/shard_map/stack | solution.py:33
  91.7 5.0 %all-to-all-start.2 = ((bf16[8,1,128,3072]{3,2,1,0:T(8,128)(2,1)}), bf16[8,1,128,3072]{3,2,1,0:T(8,128)(2,1)}, u32[]{:S(2)}, u32[]{:S(2)}) async-start(bf16[8,1,128,3072]{3,2,1,0:T(8,128)(2,1)} %stack.7), calls=%async_computation.2 | async-start | bytes 12582912 | tf_op jit(solution)/shard_map/all_to_all | solution.py:33
  96.7 0.0 collective-permute-start.1
  96.7 5.0 %convolution_convert_fusion.2 = bf16[128,1024]{1,0:T(8,128)(2,1)S(1)} fusion(bf16[1024,3072]{1,0:T(8,128)(2,1)} %bitcast.2, bf16[1,128,3072]{2,1,0:T(8,128)(2,1)S(1)} %copy-done), kind=kOutput, calls=%fused_computation.6 | convolution fusion | flops 805437440 | bytes 7340032 | tf_op jit(solution)/shard_map/dot_general | solution.py:38
  101.7 0.4 copy.8
  102.1 0.5 broadcast.161
  102.6 2.2 reduce
  104.8 0.8 reshape.220
  105.6 68.3 %all-to-all-done.2 = bf16[8,1,128,3072]{3,2,1,0:T(8,128)(2,1)} async-done(((bf16[8,1,128,3072]{3,2,1,0:T(8,128)(2,1)}), bf16[8,1,128,3072]{3,2,1,0:T(8,128)(2,1)}, u32[]{:S(2)}, u32[]{:S(2)}) %all-to-all-start.2) | async-done | bytes 6291488 | tf_op jit(solution)/shard_map/all_to_all | solution.py:33
  173.9 4.3 %all-to-all-start.1 = ((bf16[8,2,8192]{2,1,0:T(2,128)(2,1)}), bf16[8,2,8192]{2,1,0:T(2,128)(2,1)S(1)}, u32[]{:S(2)}, u32[]{:S(2)}) async-start(bf16[8,2,8192]{2,1,0:T(2,128)(2,1)} %reshape.220), calls=%async_computation.1 | async-start | bytes 524288 | tf_op jit(solution)/shard_map/all_to_all | solution.py:42
  178.2 5.0 %convolution_convert_fusion.1 = bf16[128,1024]{1,0:T(8,128)(2,1)S(1)} fusion(bf16[1024,3072]{1,0:T(8,128)(2,1)} %bitcast.11, bf16[1,128,3072]{2,1,0:T(8,128)(2,1)S(1)} %copy-done), kind=kOutput, calls=%fused_computation.5 | convolution fusion | flops 805437440 | bytes 7340032 | tf_op jit(solution)/shard_map/dot_general | solution.py:38
  183.2 0.4 copy.10
  183.6 2.2 reduce.1
  185.8 0.8 reshape.222
  186.5 0.0 all-to-all-done.1
  186.5 5.7 %all-to-all-start.3 = ((bf16[8,2,8192]{2,1,0:T(2,128)(2,1)}), bf16[8,2,8192]{2,1,0:T(2,128)(2,1)S(1)}, u32[]{:S(2)}, u32[]{:S(2)}) async-start(bf16[8,2,8192]{2,1,0:T(2,128)(2,1)} %reshape.222), calls=%async_computation.3 | async-start | bytes 524288 | tf_op jit(solution)/shard_map/all_to_all | solution.py:42
  192.3 0.0 collective-permute-done.1
  192.3 7.2 %all-to-all-done.3 = bf16[8,2,8192]{2,1,0:T(2,128)(2,1)S(1)} async-done(((bf16[8,2,8192]{2,1,0:T(2,128)(2,1)}), bf16[8,2,8192]{2,1,0:T(2,128)(2,1)S(1)}, u32[]{:S(2)}, u32[]{:S(2)}) %all-to-all-start.3) | async-done | bytes 262176 | tf_op jit(solution)/shard_map/all_to_all | solution.py:42
  199.5 0.0 copy-start.1
  199.5 4.7 %stack.8 = bf16[8,1,128,3072]{3,2,1,0:T(8,128)(2,1)} broadcast(bf16[128,3072]{1,0:T(8,128)(2,1)} %bitcast.19), dimensions={2,3} | broadcast | bytes 7077888 | tf_op jit(solution)/shard_map/stack | solution.py:33
  204.1 0.0 copy-start.3
  204.1 0.0 copy-start.2
  204.1 0.0 copy-done.1
  204.1 5.1 %all-to-all-start.4 = ((bf16[8,1,128,3072]{3,2,1,0:T(8,128)(2,1)}), bf16[8,1,128,3072]{3,2,1,0:T(8,128)(2,1)}, u32[]{:S(2)}, u32[]{:S(2)}) async-start(bf16[8,1,128,3072]{3,2,1,0:T(8,128)(2,1)} %stack.8), calls=%async_computation.4 | async-start | bytes 12582912 | tf_op jit(solution)/shard_map/all_to_all | solution.py:33
  209.3 0.0 copy-done.3
  209.3 0.6 fusion.25
  213.4 0.0 copy-done.2
  213.5 0.1 broadcast_subtract_fusion
  213.5 0.3 reshape.221
  213.8 0.5 bitcast_convert_fusion.2
  214.4 0.3 copy.19
  214.7 0.1 reshape.214
  214.8 4.3 %convolution_add_fusion.2 = f32[128,3072]{1,0:T(8,128)S(1)} fusion(bf16[1024,3072]{1,0:T(8,128)(2,1)} %bitcast.2, f32[1,128,3072]{2,1,0:T(8,128)} %param.7, f32[1,1024,1,128]{1,3,2,0:T(8,128)S(1)} %reshape.214, bf16[128,1024]{1,0:T(8,128)(2,1)S(1)} %convolution_convert_fusion.2, f32[1024]{0:T(1024)S(1)} %copy-done.2, f32[128]{0:T(128)S(1)} %get-tuple-element.7), kind=kOutput, calls=%fused_computation.3 | convolution fusion | flops 806486016 | bytes 10228224 | tf_op jit(solution)/shard_map/dot_general | solution.py:54
  219.1 1.2 reshape.223
  220.3 0.5 bitcast_convert_fusion.1
  220.8 1.1 copy.18
  221.9 1.1 reshape.215
  223.1 53.0 %all-to-all-done.4 = bf16[8,1,128,3072]{3,2,1,0:T(8,128)(2,1)} async-done(((bf16[8,1,128,3072]{3,2,1,0:T(8,128)(2,1)}), bf16[8,1,128,3072]{3,2,1,0:T(8,128)(2,1)}, u32[]{:S(2)}, u32[]{:S(2)}) %all-to-all-start.4) | async-done | bytes 6291488 | tf_op jit(solution)/shard_map/all_to_all | solution.py:33
  276.0 5.0 %convolution_convert_fusion = bf16[128,1024]{1,0:T(8,128)(2,1)S(1)} fusion(bf16[1024,3072]{1,0:T(8,128)(2,1)} %bitcast.20, bf16[1,128,3072]{2,1,0:T(8,128)(2,1)S(1)} %copy-done), kind=kOutput, calls=%fused_computation.4 | convolution fusion | flops 805437440 | bytes 7340032 | tf_op jit(solution)/shard_map/dot_general | solution.py:38
  281.0 0.4 copy.12
  281.4 2.2 reduce.2
  283.6 0.8 reshape.224
  284.4 3.6 %all-to-all-start.5 = ((bf16[8,2,8192]{2,1,0:T(2,128)(2,1)}), bf16[8,2,8192]{2,1,0:T(2,128)(2,1)S(1)}, u32[]{:S(2)}, u32[]{:S(2)}) async-start(bf16[8,2,8192]{2,1,0:T(2,128)(2,1)} %reshape.224), calls=%async_computation.5 | async-start | bytes 524288 | tf_op jit(solution)/shard_map/all_to_all | solution.py:42
  288.0 5.0 %convolution_add_fusion.1 = f32[128,3072]{1,0:T(8,128)} fusion(f32[128,3072]{1,0:T(8,128)S(1)} %convolution_add_fusion.2, bf16[1024,3072]{1,0:T(8,128)(2,1)} %bitcast.11, f32[1,1024,1,128]{1,3,2,0:T(8,128)S(1)} %reshape.215, bf16[128,1024]{1,0:T(8,128)(2,1)S(1)} %convolution_convert_fusion.1, f32[128]{0:T(128)S(1)} %get-tuple-element.6, f32[1024]{0:T(1024)S(1)} %copy-done.2), kind=kOutput, calls=%fused_computation.2 | convolution fusion | flops 806486016 | bytes 10228224 | tf_op jit(solution)/shard_map/dot_general | solution.py:54
  293.0 2.4 all-to-all-done.5
  295.4 0.3 reshape.225
  295.6 0.5 bitcast_convert_fusion
  296.2 0.3 copy.17
  296.5 0.1 reshape.216
  296.6 5.5 %fusion = f32[1,128,3072]{2,1,0:T(8,128)} fusion(f32[128,3072]{1,0:T(8,128)} %convolution_add_fusion.1, bf16[1024,3072]{1,0:T(8,128)(2,1)} %bitcast.20, f32[1,1024,1,128]{1,3,2,0:T(8,128)S(1)} %reshape.216, bf16[128,1024]{1,0:T(8,128)(2,1)S(1)} %convolution_convert_fusion, f32[128]{0:T(128)S(1)} %get-tuple-element.5, f32[1024]{0:T(1024)S(1)} %copy-done.2), kind=kOutput, calls=%fused_computation.1 | convolution fusion | flops 806486016 | bytes 10228224 | tf_op jit(solution)/shard_map/dot_general | solution.py:54
Async XLA Ops:
  4.6 5.2 %copy-start = (bf16[1,128,3072]{2,1,0:T(8,128)(2,1)S(1)}, bf16[1,128,3072]{2,1,0:T(8,128)(2,1)}, u32[]{:S(2)}) copy-start(bf16[1,128,3072]{2,1,0:T(8,128)(2,1)} %param.4) | copy-start | bytes 2359300
  4.6 83.7 %all-to-all-start = ((bf16[8,1,128,3072]{3,2,1,0:T(8,128)(2,1)}), bf16[8,1,128,3072]{3,2,1,0:T(8,128)(2,1)}, u32[]{:S(2)}, u32[]{:S(2)}) async-start(bf16[8,1,128,3072]{3,2,1,0:T(8,128)(2,1)} %stack.6), calls=%async_computation | async-start | bytes 12582912 | tf_op jit(solution)/shard_map/all_to_all | solution.py:33
  9.9 77.3 %collective-permute-start = (bf16[1,128,3072]{2,1,0:T(8,128)(2,1)S(1)}, bf16[1,128,3072]{2,1,0:T(8,128)(2,1)S(1)}, u32[]{:S(2)}, u32[]{:S(2)}) collective-permute-start(bf16[1,128,3072]{2,1,0:T(8,128)(2,1)S(1)} %copy-done), channel_id=1, source_target_pairs={{248,0},{0,8},{8,16},{16,24},{24,32},{32,40},{40,48},{48,56},{56,6... | collective-permute-start | bytes 2359304 | tf_op jit(solution)/shard_map/ppermute | solution.py:12
  91.7 82.2 %all-to-all-start.2 = ((bf16[8,1,128,3072]{3,2,1,0:T(8,128)(2,1)}), bf16[8,1,128,3072]{3,2,1,0:T(8,128)(2,1)}, u32[]{:S(2)}, u32[]{:S(2)}) async-start(bf16[8,1,128,3072]{3,2,1,0:T(8,128)(2,1)} %stack.7), calls=%async_computation.2 | async-start | bytes 12582912 | tf_op jit(solution)/shard_map/all_to_all | solution.py:33
  96.7 95.6 %collective-permute-start.1 = (bf16[1,128,3072]{2,1,0:T(8,128)(2,1)S(1)}, bf16[1,128,3072]{2,1,0:T(8,128)(2,1)}, u32[]{:S(2)}, u32[]{:S(2)}) collective-permute-start(bf16[1,128,3072]{2,1,0:T(8,128)(2,1)S(1)} %collective-permute-done), channel_id=1, source_target_pairs={{248,0},{0,8},{8,16},{16,24},{24,32},{32,40},{40,48},{48,56},{56,6... | collective-permute-start | bytes 2359304 | tf_op jit(solution)/shard_map/ppermute | solution.py:12
  173.9 12.6 %all-to-all-start.1 = ((bf16[8,2,8192]{2,1,0:T(2,128)(2,1)}), bf16[8,2,8192]{2,1,0:T(2,128)(2,1)S(1)}, u32[]{:S(2)}, u32[]{:S(2)}) async-start(bf16[8,2,8192]{2,1,0:T(2,128)(2,1)} %reshape.220), calls=%async_computation.1 | async-start | bytes 524288 | tf_op jit(solution)/shard_map/all_to_all | solution.py:42
  186.5 12.9 %all-to-all-start.3 = ((bf16[8,2,8192]{2,1,0:T(2,128)(2,1)}), bf16[8,2,8192]{2,1,0:T(2,128)(2,1)S(1)}, u32[]{:S(2)}, u32[]{:S(2)}) async-start(bf16[8,2,8192]{2,1,0:T(2,128)(2,1)} %reshape.222), calls=%async_computation.3 | async-start | bytes 524288 | tf_op jit(solution)/shard_map/all_to_all | solution.py:42
  199.5 4.7 %copy-start.1 = (bf16[8,2,8192]{2,1,0:T(2,128)(2,1)}, bf16[8,2,8192]{2,1,0:T(2,128)(2,1)S(1)}, u32[]{:S(2)}) copy-start(bf16[8,2,8192]{2,1,0:T(2,128)(2,1)S(1)} %all-to-all-done.3) | copy-start | bytes 786436
  204.1 5.2 %copy-start.3 = (f32[32]{0:T(128)S(1)}, f32[32]{0:T(128)}, u32[]{:S(2)}) copy-start(f32[32]{0:T(128)} %param.5) | copy-start | bytes 388
  204.1 9.3 %copy-start.2 = (f32[1024]{0:T(1024)S(1)}, f32[1024]{0:T(1024)}, u32[]{:S(2)}) copy-start(f32[1024]{0:T(1024)} %param.6) | copy-start | bytes 12292
  204.1 71.9 %all-to-all-start.4 = ((bf16[8,1,128,3072]{3,2,1,0:T(8,128)(2,1)}), bf16[8,1,128,3072]{3,2,1,0:T(8,128)(2,1)}, u32[]{:S(2)}, u32[]{:S(2)}) async-start(bf16[8,1,128,3072]{3,2,1,0:T(8,128)(2,1)} %stack.8), calls=%async_computation.4 | async-start | bytes 12582912 | tf_op jit(solution)/shard_map/all_to_all | solution.py:33
  284.4 11.0 %all-to-all-start.5 = ((bf16[8,2,8192]{2,1,0:T(2,128)(2,1)}), bf16[8,2,8192]{2,1,0:T(2,128)(2,1)S(1)}, u32[]{:S(2)}, u32[]{:S(2)}) async-start(bf16[8,2,8192]{2,1,0:T(2,128)(2,1)} %reshape.224), calls=%async_computation.5 | async-start | bytes 524288 | tf_op jit(solution)/shard_map/all_to_all | solution.py:42
